TPU v7x, 512 devices: a whole 4x8x8 slice. The times are simulated.
512 devices in a mesh: skill: 64 (over y_lo, x, z), tensor: 8 (over y_hi, core).
Axes of the slice: x: 4, y: 8 (y_hi: 4, y_lo: 2; y = y_hi * 2 + y_lo), z: 8, core: 2. Of those that a mesh axis runs over, the one named last changes fastest.
Arguments:
- stored_inputs: bfloat16 [64, 256, 8192], P('skill', None, 'tensor'), may hold values from -6 to 6
- stored_output_gradient: bfloat16 [64, 256, 15360], P('skill', None, 'tensor'), may hold values from -6 to 6
- training_token_index: int32 [64, 256], P('skill'), may hold values from 0 to 255
- validation_inputs: bfloat16 [64, 512, 8192], P('skill', None, 'tensor'), may hold values from -6 to 6
- validation_output_gradient: bfloat16 [64, 512, 15360], P('skill', None, 'tensor'), may hold values from -6 to 6
- validation_row_skill: int32 [64, 512], P('skill'), may hold values from 0 to 63
- adapter_down_init: bfloat16 [64, 8192, 64], P('skill', 'tensor'), may hold values from -0.0625 to 0.0625
Outputs:
- own_delta: float32 [64, 17], P('skill')
- other_delta: float32 [64, 17], P('skill')
All inputs are finite; a program needn't handle non-finite values.
Results may differ from a plain program's by a relative error of at most 0.0042.
Values may be sent and summed in bfloat16 or wider, within the bound.
A program may use at most 64 MiB of HBM per device.

v0:
```python
import jax
import jax.numpy as jnp
from jax import lax
from jax.sharding import PartitionSpec as P


def from_behind(block, axis, distance):
    devices = range(lax.axis_size(axis))
    route = [((i - distance) % len(devices), i) for i in devices]
    return lax.ppermute(block, axis, route)


def evaluate(down_piece, up_piece, valid_act, valid_cot, own_mask, other_mask):
    partial_value = jnp.dot(valid_act, down_piece, preferred_element_type=jnp.float32)
    summed = lax.psum(partial_value, "tensor")
    cot_proj = lax.dot_general(
        valid_cot, up_piece, (((1,), (1,)), ((), ())), preferred_element_type=jnp.float32
    )
    row_change = jnp.sum(summed * cot_proj, axis=1)
    return jnp.stack([jnp.sum(row_change * own_mask), jnp.sum(row_change * other_mask)])


def on_device(
    stored_inputs,
    stored_output_gradient,
    training_token_index,
    validation_inputs,
    validation_output_gradient,
    validation_row_skill,
    adapter_down_init,
):
    chosen = training_token_index[0]
    train_act = jnp.take(stored_inputs[0], chosen, axis=0)
    train_cot = jnp.take(stored_output_gradient[0], chosen, axis=0)
    local_down_factor = adapter_down_init[0]
    partial_value = jnp.dot(train_act, local_down_factor, preferred_element_type=jnp.float32)
    proj = lax.psum(partial_value, "tensor").astype(jnp.bfloat16)
    product = lax.dot_general(
        proj, train_cot, (((0,), (0,)), ((), ())), preferred_element_type=jnp.float32
    )
    up_local = (product * (-1.0 / chosen.shape[0])).astype(jnp.bfloat16)
    valid_act = validation_inputs[0]
    valid_cot = validation_output_gradient[0]
    labels = validation_row_skill[0]
    my_skill = lax.axis_index("skill")
    own_mask = (labels == my_skill).astype(jnp.float32)
    other_mask = 1.0 - own_mask

    def score(down_piece, up_piece):
        return evaluate(down_piece, up_piece, valid_act, valid_cot, own_mask, other_mask)

    reach_count = lax.axis_size("skill") // 8
    column_count = 2 * reach_count + 1
    scores = jnp.zeros((column_count, 2), jnp.float32)
    first_down, first_up = from_behind((local_down_factor, up_local), "skill", reach_count)

    def advance(column, carry):
        held_down, held_up, table = carry
        table = table.at[column].set(score(held_down, held_up))
        held_down, held_up = from_behind((held_down, held_up), "skill", -1)
        return (held_down, held_up, table)

    last_down, last_up, scores = lax.fori_loop(
        0, column_count - 1, advance, (first_down, first_up, scores)
    )
    scores = scores.at[column_count - 1].set(score(last_down, last_up))
    totals = lax.psum(scores, "tensor")
    own_count = jnp.maximum(jnp.sum(own_mask), 1.0)
    other_count = jnp.maximum(jnp.sum(other_mask), 1.0)
    own_delta = (totals[:, 0] / own_count)[None, :]
    other_delta = (totals[:, 1] / other_count)[None, :]
    return (own_delta, other_delta)


def solution(mesh):
    in_specs = (
        P("skill", None, "tensor"),
        P("skill", None, "tensor"),
        P("skill", None),
        P("skill", None, "tensor"),
        P("skill", None, "tensor"),
        P("skill", None),
        P("skill", "tensor", None),
    )
    out_specs = (P("skill", None), P("skill", None))
    return jax.shard_map(
        on_device, mesh=mesh, in_specs=in_specs, out_specs=out_specs, check_vma=False
    )
```

profile of v0, /device:TPU:2, one launch (start us, length us, event | category | flops | bytes accessed | tf_op | source)
XLA Modules:
  0.0 1527.6 jit_solution(34875046202805492)
XLA Ops:
  12.5 32.0 %psum.32 = bf16[256,64]{1,0:T(8,128)(2,1)S(1)} all-reduce(f32[256,64]{1,0:T(8,128)S(1)} %fusion.4), channel_id=1, replica_groups=mesh['skill'=64,'tensor'=8] {'tensor'}, use_global_device_ids=true, to_apply=%region_0.1 | all-reduce | flops 16384 | bytes 98304 | tf_op jit(solution)/shard_map/psum | solution.py:37
  55.9 6.8 collective-permute-done.2
  62.7 1346.3 %while.19 = (s32[]{:T(128)}, bf16[1024,64]{1,0:T(8,128)(2,1)}, bf16[64,1920]{1,0:T(8,128)(2,1)}, f32[17,2]{1,0:T(8,128)S(1)}, bf16[512,1024]{1,0:T(8,128)(2,1)},...) while((s32[]{:T(128)}, bf16[1024,64]{1,0:T(8,128)(2,1)}, ...), condition=%wide.region_7.8_spmd, body=%wide.region_1.7_spmd.sunk | while | flops 193037824 | bytes 6709567 | solution.py:63
  66.0 11.7 collective-permute-start
  81.8 63.7 %all-reduce.5.cloned.1.call-done = f32[512,64]{0,1:T(8,128)} async-done(((f32[512,64]{0,1:T(8,128)}), f32[512,64]{0,1:T(8,128)}) %all-reduce.5.cloned.1.call-update) | async-done | bytes 131088 | tf_op jit(solution)/shard_map/while/body/eval_jaxpr/psum | solution.py:15
  153.1 5.9 collective-permute-start
  163.8 65.9 %all-reduce.5.cloned.1.call-done = f32[512,64]{0,1:T(8,128)} async-done(((f32[512,64]{0,1:T(8,128)}), f32[512,64]{0,1:T(8,128)}) %all-reduce.5.cloned.1.call-update) | async-done | bytes 131088 | tf_op jit(solution)/shard_map/while/body/eval_jaxpr/psum | solution.py:15
  237.3 5.9 collective-permute-start
  248.0 65.9 %all-reduce.5.cloned.1.call-done = f32[512,64]{0,1:T(8,128)} async-done(((f32[512,64]{0,1:T(8,128)}), f32[512,64]{0,1:T(8,128)}) %all-reduce.5.cloned.1.call-update) | async-done | bytes 131088 | tf_op jit(solution)/shard_map/while/body/eval_jaxpr/psum | solution.py:15
  332.1 65.5 %all-reduce.5.cloned.1.call-done = f32[512,64]{0,1:T(8,128)} async-done(((f32[512,64]{0,1:T(8,128)}), f32[512,64]{0,1:T(8,128)}) %all-reduce.5.cloned.1.call-update) | async-done | bytes 131088 | tf_op jit(solution)/shard_map/while/body/eval_jaxpr/psum | solution.py:15
  405.2 5.9 collective-permute-start
  415.9 65.5 %all-reduce.5.cloned.1.call-done = f32[512,64]{0,1:T(8,128)} async-done(((f32[512,64]{0,1:T(8,128)}), f32[512,64]{0,1:T(8,128)}) %all-reduce.5.cloned.1.call-update) | async-done | bytes 131088 | tf_op jit(solution)/shard_map/while/body/eval_jaxpr/psum | solution.py:15
  489.0 5.9 collective-permute-start
  499.7 65.5 %all-reduce.5.cloned.1.call-done = f32[512,64]{0,1:T(8,128)} async-done(((f32[512,64]{0,1:T(8,128)}), f32[512,64]{0,1:T(8,128)}) %all-reduce.5.cloned.1.call-update) | async-done | bytes 131088 | tf_op jit(solution)/shard_map/while/body/eval_jaxpr/psum | solution.py:15
  583.5 65.8 %all-reduce.5.cloned.1.call-done = f32[512,64]{0,1:T(8,128)} async-done(((f32[512,64]{0,1:T(8,128)}), f32[512,64]{0,1:T(8,128)}) %all-reduce.5.cloned.1.call-update) | async-done | bytes 131088 | tf_op jit(solution)/shard_map/while/body/eval_jaxpr/psum | solution.py:15
  656.9 5.9 collective-permute-start
  667.6 65.8 %all-reduce.5.cloned.1.call-done = f32[512,64]{0,1:T(8,128)} async-done(((f32[512,64]{0,1:T(8,128)}), f32[512,64]{0,1:T(8,128)}) %all-reduce.5.cloned.1.call-update) | async-done | bytes 131088 | tf_op jit(solution)/shard_map/while/body/eval_jaxpr/psum | solution.py:15
  741.0 5.9 collective-permute-start
  751.7 65.8 %all-reduce.5.cloned.1.call-done = f32[512,64]{0,1:T(8,128)} async-done(((f32[512,64]{0,1:T(8,128)}), f32[512,64]{0,1:T(8,128)}) %all-reduce.5.cloned.1.call-update) | async-done | bytes 131088 | tf_op jit(solution)/shard_map/while/body/eval_jaxpr/psum | solution.py:15
  835.8 65.6 %all-reduce.5.cloned.1.call-done = f32[512,64]{0,1:T(8,128)} async-done(((f32[512,64]{0,1:T(8,128)}), f32[512,64]{0,1:T(8,128)}) %all-reduce.5.cloned.1.call-update) | async-done | bytes 131088 | tf_op jit(solution)/shard_map/while/body/eval_jaxpr/psum | solution.py:15
  908.9 5.9 collective-permute-start
  919.6 65.8 %all-reduce.5.cloned.1.call-done = f32[512,64]{0,1:T(8,128)} async-done(((f32[512,64]{0,1:T(8,128)}), f32[512,64]{0,1:T(8,128)}) %all-reduce.5.cloned.1.call-update) | async-done | bytes 131088 | tf_op jit(solution)/shard_map/while/body/eval_jaxpr/psum | solution.py:15
  1003.7 65.5 %all-reduce.5.cloned.1.call-done = f32[512,64]{0,1:T(8,128)} async-done(((f32[512,64]{0,1:T(8,128)}), f32[512,64]{0,1:T(8,128)}) %all-reduce.5.cloned.1.call-update) | async-done | bytes 131088 | tf_op jit(solution)/shard_map/while/body/eval_jaxpr/psum | solution.py:15
  1087.5 65.8 %all-reduce.5.cloned.1.call-done = f32[512,64]{0,1:T(8,128)} async-done(((f32[512,64]{0,1:T(8,128)}), f32[512,64]{0,1:T(8,128)}) %all-reduce.5.cloned.1.call-update) | async-done | bytes 131088 | tf_op jit(solution)/shard_map/while/body/eval_jaxpr/psum | solution.py:15
  1160.9 5.9 collective-permute-start
  1171.6 65.5 %all-reduce.5.cloned.1.call-done = f32[512,64]{0,1:T(8,128)} async-done(((f32[512,64]{0,1:T(8,128)}), f32[512,64]{0,1:T(8,128)}) %all-reduce.5.cloned.1.call-update) | async-done | bytes 131088 | tf_op jit(solution)/shard_map/while/body/eval_jaxpr/psum | solution.py:15
  1244.7 5.9 collective-permute-start
  1255.4 65.6 %all-reduce.5.cloned.1.call-done = f32[512,64]{0,1:T(8,128)} async-done(((f32[512,64]{0,1:T(8,128)}), f32[512,64]{0,1:T(8,128)}) %all-reduce.5.cloned.1.call-update) | async-done | bytes 131088 | tf_op jit(solution)/shard_map/while/body/eval_jaxpr/psum | solution.py:15
  1328.6 5.9 collective-permute-start
  1339.2 65.5 %all-reduce.5.cloned.1.call-done = f32[512,64]{0,1:T(8,128)} async-done(((f32[512,64]{0,1:T(8,128)}), f32[512,64]{0,1:T(8,128)}) %all-reduce.5.cloned.1.call-update) | async-done | bytes 131088 | tf_op jit(solution)/shard_map/while/body/eval_jaxpr/psum | solution.py:15
  1413.1 74.8 %all-reduce.3.cloned.1.call-done = f32[512,64]{0,1:T(8,128)} async-done(((f32[512,64]{0,1:T(8,128)}), f32[512,64]{0,1:T(8,128)}) %all-reduce.3.cloned.1.call-update) | async-done | bytes 131088 | tf_op jit(solution)/shard_map/psum | solution.py:15
  1490.9 27.6 %psum.34 = f32[17,2]{1,0:T(8,128)S(1)} all-reduce(f32[17,2]{1,0:T(8,128)S(1)} %scatter.7), channel_id=1, replica_groups=mesh['skill'=64,'tensor'=8] {'tensor'}, use_global_device_ids=true, to_apply=%region_12.13 | all-reduce | flops 34 | bytes 272 | tf_op jit(solution)/shard_map/psum | solution.py:67
  (247 shorter events, 250.4 us)
Async XLA Ops:
  62.7 82.8 %all-reduce.5.cloned.1.call-start = ((), (), s32[]{:S(2)}) async-start(), calls=%async_computation.1 | async-start | bytes 262144 | tf_op jit(solution)/shard_map/while/body/eval_jaxpr/psum | solution.py:15
  66.0 83.7 %collective-permute-start = (bf16[1024,64]{1,0:T(8,128)(2,1)S(1)}, bf16[1024,64]{1,0:T(8,128)(2,1)}, u32[]{:S(2)}, u32[]{:S(2)}) collective-permute-start(bf16[1024,64]{1,0:T(8,128)(2,1)S(1)} %copy.18), channel_id=1, source_target_pairs={{8,0},{16,8},{24,16},{32,24},{40,32},{48,40},{56,48},{64,56},{72,6... | collective-permute-start | bytes 393224 | tf_op jit(solution)/shard_map/while/body/eval_jaxpr/ppermute | solution.py:10
  149.8 79.9 %all-reduce.5.cloned.1.call-start = ((), (), s32[]{:S(2)}) async-start(), calls=%async_computation.1 | async-start | bytes 262144 | tf_op jit(solution)/shard_map/while/body/eval_jaxpr/psum | solution.py:15
  153.1 80.8 %collective-permute-start = (bf16[1024,64]{1,0:T(8,128)(2,1)S(1)}, bf16[1024,64]{1,0:T(8,128)(2,1)}, u32[]{:S(2)}, u32[]{:S(2)}) collective-permute-start(bf16[1024,64]{1,0:T(8,128)(2,1)S(1)} %copy.18), channel_id=1, source_target_pairs={{8,0},{16,8},{24,16},{32,24},{40,32},{48,40},{56,48},{64,56},{72,6... | collective-permute-start | bytes 393224 | tf_op jit(solution)/shard_map/while/body/eval_jaxpr/ppermute | solution.py:10
  233.9 79.9 %all-reduce.5.cloned.1.call-start = ((), (), s32[]{:S(2)}) async-start(), calls=%async_computation.1 | async-start | bytes 262144 | tf_op jit(solution)/shard_map/while/body/eval_jaxpr/psum | solution.py:15
  237.3 80.8 %collective-permute-start = (bf16[1024,64]{1,0:T(8,128)(2,1)S(1)}, bf16[1024,64]{1,0:T(8,128)(2,1)}, u32[]{:S(2)}, u32[]{:S(2)}) collective-permute-start(bf16[1024,64]{1,0:T(8,128)(2,1)S(1)} %copy.18), channel_id=1, source_target_pairs={{8,0},{16,8},{24,16},{32,24},{40,32},{48,40},{56,48},{64,56},{72,6... | collective-permute-start | bytes 393224 | tf_op jit(solution)/shard_map/while/body/eval_jaxpr/ppermute | solution.py:10
  318.1 79.5 %all-reduce.5.cloned.1.call-start = ((), (), s32[]{:S(2)}) async-start(), calls=%async_computation.1 | async-start | bytes 262144 | tf_op jit(solution)/shard_map/while/body/eval_jaxpr/psum | solution.py:15
  321.5 80.4 %collective-permute-start = (bf16[1024,64]{1,0:T(8,128)(2,1)S(1)}, bf16[1024,64]{1,0:T(8,128)(2,1)}, u32[]{:S(2)}, u32[]{:S(2)}) collective-permute-start(bf16[1024,64]{1,0:T(8,128)(2,1)S(1)} %copy.18), channel_id=1, source_target_pairs={{8,0},{16,8},{24,16},{32,24},{40,32},{48,40},{56,48},{64,56},{72,6... | collective-permute-start | bytes 393224 | tf_op jit(solution)/shard_map/while/body/eval_jaxpr/ppermute | solution.py:10
  401.9 79.5 %all-reduce.5.cloned.1.call-start = ((), (), s32[]{:S(2)}) async-start(), calls=%async_computation.1 | async-start | bytes 262144 | tf_op jit(solution)/shard_map/while/body/eval_jaxpr/psum | solution.py:15
  405.2 80.4 %collective-permute-start = (bf16[1024,64]{1,0:T(8,128)(2,1)S(1)}, bf16[1024,64]{1,0:T(8,128)(2,1)}, u32[]{:S(2)}, u32[]{:S(2)}) collective-permute-start(bf16[1024,64]{1,0:T(8,128)(2,1)S(1)} %copy.18), channel_id=1, source_target_pairs={{8,0},{16,8},{24,16},{32,24},{40,32},{48,40},{56,48},{64,56},{72,6... | collective-permute-start | bytes 393224 | tf_op jit(solution)/shard_map/while/body/eval_jaxpr/ppermute | solution.py:10
  485.7 79.5 %all-reduce.5.cloned.1.call-start = ((), (), s32[]{:S(2)}) async-start(), calls=%async_computation.1 | async-start | bytes 262144 | tf_op jit(solution)/shard_map/while/body/eval_jaxpr/psum | solution.py:15
  489.0 80.4 %collective-permute-start = (bf16[1024,64]{1,0:T(8,128)(2,1)S(1)}, bf16[1024,64]{1,0:T(8,128)(2,1)}, u32[]{:S(2)}, u32[]{:S(2)}) collective-permute-start(bf16[1024,64]{1,0:T(8,128)(2,1)S(1)} %copy.18), channel_id=1, source_target_pairs={{8,0},{16,8},{24,16},{32,24},{40,32},{48,40},{56,48},{64,56},{72,6... | collective-permute-start | bytes 393224 | tf_op jit(solution)/shard_map/while/body/eval_jaxpr/ppermute | solution.py:10
  569.5 79.8 %all-reduce.5.cloned.1.call-start = ((), (), s32[]{:S(2)}) async-start(), calls=%async_computation.1 | async-start | bytes 262144 | tf_op jit(solution)/shard_map/while/body/eval_jaxpr/psum | solution.py:15
  572.8 80.7 %collective-permute-start = (bf16[1024,64]{1,0:T(8,128)(2,1)S(1)}, bf16[1024,64]{1,0:T(8,128)(2,1)}, u32[]{:S(2)}, u32[]{:S(2)}) collective-permute-start(bf16[1024,64]{1,0:T(8,128)(2,1)S(1)} %copy.18), channel_id=1, source_target_pairs={{8,0},{16,8},{24,16},{32,24},{40,32},{48,40},{56,48},{64,56},{72,6... | collective-permute-start | bytes 393224 | tf_op jit(solution)/shard_map/while/body/eval_jaxpr/ppermute | solution.py:10
  653.6 79.8 %all-reduce.5.cloned.1.call-start = ((), (), s32[]{:S(2)}) async-start(), calls=%async_computation.1 | async-start | bytes 262144 | tf_op jit(solution)/shard_map/while/body/eval_jaxpr/psum | solution.py:15
  656.9 80.7 %collective-permute-start = (bf16[1024,64]{1,0:T(8,128)(2,1)S(1)}, bf16[1024,64]{1,0:T(8,128)(2,1)}, u32[]{:S(2)}, u32[]{:S(2)}) collective-permute-start(bf16[1024,64]{1,0:T(8,128)(2,1)S(1)} %copy.18), channel_id=1, source_target_pairs={{8,0},{16,8},{24,16},{32,24},{40,32},{48,40},{56,48},{64,56},{72,6... | collective-permute-start | bytes 393224 | tf_op jit(solution)/shard_map/while/body/eval_jaxpr/ppermute | solution.py:10
  737.7 79.8 %all-reduce.5.cloned.1.call-start = ((), (), s32[]{:S(2)}) async-start(), calls=%async_computation.1 | async-start | bytes 262144 | tf_op jit(solution)/shard_map/while/body/eval_jaxpr/psum | solution.py:15
  741.0 80.7 %collective-permute-start = (bf16[1024,64]{1,0:T(8,128)(2,1)S(1)}, bf16[1024,64]{1,0:T(8,128)(2,1)}, u32[]{:S(2)}, u32[]{:S(2)}) collective-permute-start(bf16[1024,64]{1,0:T(8,128)(2,1)S(1)} %copy.18), channel_id=1, source_target_pairs={{8,0},{16,8},{24,16},{32,24},{40,32},{48,40},{56,48},{64,56},{72,6... | collective-permute-start | bytes 393224 | tf_op jit(solution)/shard_map/while/body/eval_jaxpr/ppermute | solution.py:10
  821.7 79.6 %all-reduce.5.cloned.1.call-start = ((), (), s32[]{:S(2)}) async-start(), calls=%async_computation.1 | async-start | bytes 262144 | tf_op jit(solution)/shard_map/while/body/eval_jaxpr/psum | solution.py:15
  825.1 80.5 %collective-permute-start = (bf16[1024,64]{1,0:T(8,128)(2,1)S(1)}, bf16[1024,64]{1,0:T(8,128)(2,1)}, u32[]{:S(2)}, u32[]{:S(2)}) collective-permute-start(bf16[1024,64]{1,0:T(8,128)(2,1)S(1)} %copy.18), channel_id=1, source_target_pairs={{8,0},{16,8},{24,16},{32,24},{40,32},{48,40},{56,48},{64,56},{72,6... | collective-permute-start | bytes 393224 | tf_op jit(solution)/shard_map/while/body/eval_jaxpr/ppermute | solution.py:10
  905.6 79.8 %all-reduce.5.cloned.1.call-start = ((), (), s32[]{:S(2)}) async-start(), calls=%async_computation.1 | async-start | bytes 262144 | tf_op jit(solution)/shard_map/while/body/eval_jaxpr/psum | solution.py:15
  908.9 80.7 %collective-permute-start = (bf16[1024,64]{1,0:T(8,128)(2,1)S(1)}, bf16[1024,64]{1,0:T(8,128)(2,1)}, u32[]{:S(2)}, u32[]{:S(2)}) collective-permute-start(bf16[1024,64]{1,0:T(8,128)(2,1)S(1)} %copy.18), channel_id=1, source_target_pairs={{8,0},{16,8},{24,16},{32,24},{40,32},{48,40},{56,48},{64,56},{72,6... | collective-permute-start | bytes 393224 | tf_op jit(solution)/shard_map/while/body/eval_jaxpr/ppermute | solution.py:10
  989.7 79.5 %all-reduce.5.cloned.1.call-start = ((), (), s32[]{:S(2)}) async-start(), calls=%async_computation.1 | async-start | bytes 262144 | tf_op jit(solution)/shard_map/while/body/eval_jaxpr/psum | solution.py:15
  993.0 80.4 %collective-permute-start = (bf16[1024,64]{1,0:T(8,128)(2,1)S(1)}, bf16[1024,64]{1,0:T(8,128)(2,1)}, u32[]{:S(2)}, u32[]{:S(2)}) collective-permute-start(bf16[1024,64]{1,0:T(8,128)(2,1)S(1)} %copy.18), channel_id=1, source_target_pairs={{8,0},{16,8},{24,16},{32,24},{40,32},{48,40},{56,48},{64,56},{72,6... | collective-permute-start | bytes 393224 | tf_op jit(solution)/shard_map/while/body/eval_jaxpr/ppermute | solution.py:10
  1073.5 79.8 %all-reduce.5.cloned.1.call-start = ((), (), s32[]{:S(2)}) async-start(), calls=%async_computation.1 | async-start | bytes 262144 | tf_op jit(solution)/shard_map/while/body/eval_jaxpr/psum | solution.py:15
  1076.8 80.7 %collective-permute-start = (bf16[1024,64]{1,0:T(8,128)(2,1)S(1)}, bf16[1024,64]{1,0:T(8,128)(2,1)}, u32[]{:S(2)}, u32[]{:S(2)}) collective-permute-start(bf16[1024,64]{1,0:T(8,128)(2,1)S(1)} %copy.18), channel_id=1, source_target_pairs={{8,0},{16,8},{24,16},{32,24},{40,32},{48,40},{56,48},{64,56},{72,6... | collective-permute-start | bytes 393224 | tf_op jit(solution)/shard_map/while/body/eval_jaxpr/ppermute | solution.py:10
  1157.6 79.5 %all-reduce.5.cloned.1.call-start = ((), (), s32[]{:S(2)}) async-start(), calls=%async_computation.1 | async-start | bytes 262144 | tf_op jit(solution)/shard_map/while/body/eval_jaxpr/psum | solution.py:15
  1160.9 80.4 %collective-permute-start = (bf16[1024,64]{1,0:T(8,128)(2,1)S(1)}, bf16[1024,64]{1,0:T(8,128)(2,1)}, u32[]{:S(2)}, u32[]{:S(2)}) collective-permute-start(bf16[1024,64]{1,0:T(8,128)(2,1)S(1)} %copy.18), channel_id=1, source_target_pairs={{8,0},{16,8},{24,16},{32,24},{40,32},{48,40},{56,48},{64,56},{72,6... | collective-permute-start | bytes 393224 | tf_op jit(solution)/shard_map/while/body/eval_jaxpr/ppermute | solution.py:10
  1241.3 79.6 %all-reduce.5.cloned.1.call-start = ((), (), s32[]{:S(2)}) async-start(), calls=%async_computation.1 | async-start | bytes 262144 | tf_op jit(solution)/shard_map/while/body/eval_jaxpr/psum | solution.py:15
  1244.7 80.5 %collective-permute-start = (bf16[1024,64]{1,0:T(8,128)(2,1)S(1)}, bf16[1024,64]{1,0:T(8,128)(2,1)}, u32[]{:S(2)}, u32[]{:S(2)}) collective-permute-start(bf16[1024,64]{1,0:T(8,128)(2,1)S(1)} %copy.18), channel_id=1, source_target_pairs={{8,0},{16,8},{24,16},{32,24},{40,32},{48,40},{56,48},{64,56},{72,6... | collective-permute-start | bytes 393224 | tf_op jit(solution)/shard_map/while/body/eval_jaxpr/ppermute | solution.py:10
  1325.2 79.5 %all-reduce.5.cloned.1.call-start = ((), (), s32[]{:S(2)}) async-start(), calls=%async_computation.1 | async-start | bytes 262144 | tf_op jit(solution)/shard_map/while/body/eval_jaxpr/psum | solution.py:15
  1328.6 80.4 %collective-permute-start = (bf16[1024,64]{1,0:T(8,128)(2,1)S(1)}, bf16[1024,64]{1,0:T(8,128)(2,1)}, u32[]{:S(2)}, u32[]{:S(2)}) collective-permute-start(bf16[1024,64]{1,0:T(8,128)(2,1)S(1)} %copy.18), channel_id=1, source_target_pairs={{8,0},{16,8},{24,16},{32,24},{40,32},{48,40},{56,48},{64,56},{72,6... | collective-permute-start | bytes 393224 | tf_op jit(solution)/shard_map/while/body/eval_jaxpr/ppermute | solution.py:10
  (24 other events, 1366.9 us)
Sparse Core Ops, SparseCore 0:
  66.7 78.7 all-reduce.4
  153.8 75.8 all-reduce.4
  237.9 75.8 all-reduce.4
  321.8 75.7 all-reduce.4
  405.6 75.7 all-reduce.4
  489.4 75.7 all-reduce.4
  573.5 75.7 all-reduce.4
  657.6 75.7 all-reduce.4
  741.6 75.7 all-reduce.4
  825.4 75.8 all-reduce.4
  909.6 75.7 all-reduce.4
  993.4 75.7 all-reduce.4
  1077.5 75.7 all-reduce.4
  1161.3 75.7 all-reduce.4
  1245.0 75.8 all-reduce.4
  1328.9 75.7 all-reduce.4
Sparse Core Ops, SparseCore 1:
  1412.4 75.5 all-reduce.2
where the time goes:
time: 1530 us
  waiting for transfers between devices  1130 us (74%)
  starting transfers between devices  157 us (10%)
  matrix products  69.7 us (5%)
  blocking collectives  59.5 us (4%)
  other arithmetic  57.7 us (4%)
  local copies, waits for them, and re-layouts  36 us (2%)
  between operations  16.6 us (1%)
    psum x17, waiting for transfers between devices, evaluate(): summed = lax.psum(partial_value, 'tensor')  1120 us
    ppermute x34, starting transfers between devices, from_behind(): return lax.ppermute(block, axis, route)  156 us
    another operation x33, other arithmetic  42.9 us
    dot_general x17, matrix products, evaluate(): jnp.dot(valid_act, down_piece, preferred_element_type=jnp.float32)  39.4 us
    psum x1, blocking collectives, on_device(): proj = lax.psum(partial_value, 'tensor').astype(jnp.bfloat16)  32 us
  transfers between devices with their start and end apart: 51, of which 18 were waited for; matrix products, arithmetic and copies ran while one was open for 6% of the time, Pallas kernels for 0%

commit v1 on v0

--- a/solution.py
+++ b/solution.py
@@ -34,7 +34,7 @@
     train_cot = jnp.take(stored_output_gradient[0], chosen, axis=0)
     local_down_factor = adapter_down_init[0]
     partial_value = jnp.dot(train_act, local_down_factor, preferred_element_type=jnp.float32)
-    proj = lax.psum(partial_value, "tensor").astype(jnp.bfloat16)
+    proj = jnp.sum(lax.all_gather(partial_value, "tensor"), axis=0).astype(jnp.bfloat16)
     product = lax.dot_general(
         proj, train_cot, (((0,), (0,)), ((), ())), preferred_element_type=jnp.float32
     )

time: 1530 us -> 1520 us (level)
    psum x1 -> x0, blocking collectives: 32 us -> none  [on_device(): proj = lax.psum(partial_value, 'tensor').astype(jnp.bfloat16)]
    all_gather x0 -> x1, blocking collectives: none -> 17.9 us  [on_device(): lax.all_gather(partial_value, 'tensor')]
where the time goes in v1:
time: 1520 us
  waiting for transfers between devices  1130 us (74%)
  starting transfers between devices  157 us (10%)
  matrix products  69.9 us (5%)
  other arithmetic  57.9 us (4%)
  blocking collectives  45.4 us (3%)
  local copies, waits for them, and re-layouts  36.2 us (2%)
  between operations  16.6 us (1%)
    psum x17, waiting for transfers between devices, evaluate(): summed = lax.psum(partial_value, 'tensor')  1120 us
    ppermute x34, starting transfers between devices, from_behind(): return lax.ppermute(block, axis, route)  156 us
    another operation x33, other arithmetic  42.9 us
    dot_general x17, matrix products, evaluate(): jnp.dot(valid_act, down_piece, preferred_element_type=jnp.float32)  39.4 us
  transfers between devices with their start and end apart: 51, of which 18 were waited for; matrix products, arithmetic and copies ran while one was open for 6% of the time, Pallas kernels for 0%

profile of v1, /device:TPU:2, one launch (start us, length us, event | category | flops | bytes accessed | tf_op | source)
XLA Modules:
  0.0 1517.2 jit_solution(3457675725591555926)
XLA Ops:
  12.5 17.9 %all-gather = f32[2048,64]{0,1:T(8,128)S(1)} all-gather(f32[256,64]{0,1:T(8,128)S(1)} %fusion.4), channel_id=2, replica_groups=mesh['skill'=64,'tensor'=8] {'tensor'}, dimensions={0}, use_global_device_ids=true | all-gather | bytes 589824 | tf_op jit(solution)/shard_map/all_gather | solution.py:37
  42.2 10.6 collective-permute-done.2
  52.8 1345.8 %while.19 = (s32[]{:T(128)}, bf16[1024,64]{1,0:T(8,128)(2,1)}, bf16[64,1920]{1,0:T(8,128)(2,1)}, f32[17,2]{1,0:T(8,128)S(1)}, bf16[512,1024]{1,0:T(8,128)(2,1)},...) while((s32[]{:T(128)}, bf16[1024,64]{1,0:T(8,128)(2,1)}, ...), condition=%wide.region_7.8_spmd, body=%wide.region_1.7_spmd.sunk | while | flops 193037824 | bytes 6709567 | solution.py:63
  56.2 11.7 collective-permute-start
  72.0 63.2 %all-reduce.5.cloned.1.call-done = f32[512,64]{0,1:T(8,128)} async-done(((f32[512,64]{0,1:T(8,128)}), f32[512,64]{0,1:T(8,128)}) %all-reduce.5.cloned.1.call-update) | async-done | bytes 131088 | tf_op jit(solution)/shard_map/while/body/eval_jaxpr/psum | solution.py:15
  142.8 5.9 collective-permute-start
  153.4 65.8 %all-reduce.5.cloned.1.call-done = f32[512,64]{0,1:T(8,128)} async-done(((f32[512,64]{0,1:T(8,128)}), f32[512,64]{0,1:T(8,128)}) %all-reduce.5.cloned.1.call-update) | async-done | bytes 131088 | tf_op jit(solution)/shard_map/while/body/eval_jaxpr/psum | solution.py:15
  226.9 5.9 collective-permute-start
  237.5 65.9 %all-reduce.5.cloned.1.call-done = f32[512,64]{0,1:T(8,128)} async-done(((f32[512,64]{0,1:T(8,128)}), f32[512,64]{0,1:T(8,128)}) %all-reduce.5.cloned.1.call-update) | async-done | bytes 131088 | tf_op jit(solution)/shard_map/while/body/eval_jaxpr/psum | solution.py:15
  321.7 65.5 %all-reduce.5.cloned.1.call-done = f32[512,64]{0,1:T(8,128)} async-done(((f32[512,64]{0,1:T(8,128)}), f32[512,64]{0,1:T(8,128)}) %all-reduce.5.cloned.1.call-update) | async-done | bytes 131088 | tf_op jit(solution)/shard_map/while/body/eval_jaxpr/psum | solution.py:15
  394.8 5.9 collective-permute-start
  405.5 65.5 %all-reduce.5.cloned.1.call-done = f32[512,64]{0,1:T(8,128)} async-done(((f32[512,64]{0,1:T(8,128)}), f32[512,64]{0,1:T(8,128)}) %all-reduce.5.cloned.1.call-update) | async-done | bytes 131088 | tf_op jit(solution)/shard_map/while/body/eval_jaxpr/psum | solution.py:15
  478.6 5.9 collective-permute-start
  489.3 65.5 %all-reduce.5.cloned.1.call-done = f32[512,64]{0,1:T(8,128)} async-done(((f32[512,64]{0,1:T(8,128)}), f32[512,64]{0,1:T(8,128)}) %all-reduce.5.cloned.1.call-update) | async-done | bytes 131088 | tf_op jit(solution)/shard_map/while/body/eval_jaxpr/psum | solution.py:15
  573.1 65.8 %all-reduce.5.cloned.1.call-done = f32[512,64]{0,1:T(8,128)} async-done(((f32[512,64]{0,1:T(8,128)}), f32[512,64]{0,1:T(8,128)}) %all-reduce.5.cloned.1.call-update) | async-done | bytes 131088 | tf_op jit(solution)/shard_map/while/body/eval_jaxpr/psum | solution.py:15
  646.5 5.9 collective-permute-start
  657.2 65.8 %all-reduce.5.cloned.1.call-done = f32[512,64]{0,1:T(8,128)} async-done(((f32[512,64]{0,1:T(8,128)}), f32[512,64]{0,1:T(8,128)}) %all-reduce.5.cloned.1.call-update) | async-done | bytes 131088 | tf_op jit(solution)/shard_map/while/body/eval_jaxpr/psum | solution.py:15
  730.6 5.9 collective-permute-start
  741.2 65.8 %all-reduce.5.cloned.1.call-done = f32[512,64]{0,1:T(8,128)} async-done(((f32[512,64]{0,1:T(8,128)}), f32[512,64]{0,1:T(8,128)}) %all-reduce.5.cloned.1.call-update) | async-done | bytes 131088 | tf_op jit(solution)/shard_map/while/body/eval_jaxpr/psum | solution.py:15
  825.3 65.6 %all-reduce.5.cloned.1.call-done = f32[512,64]{0,1:T(8,128)} async-done(((f32[512,64]{0,1:T(8,128)}), f32[512,64]{0,1:T(8,128)}) %all-reduce.5.cloned.1.call-update) | async-done | bytes 131088 | tf_op jit(solution)/shard_map/while/body/eval_jaxpr/psum | solution.py:15
  898.5 5.9 collective-permute-start
  909.2 65.8 %all-reduce.5.cloned.1.call-done = f32[512,64]{0,1:T(8,128)} async-done(((f32[512,64]{0,1:T(8,128)}), f32[512,64]{0,1:T(8,128)}) %all-reduce.5.cloned.1.call-update) | async-done | bytes 131088 | tf_op jit(solution)/shard_map/while/body/eval_jaxpr/psum | solution.py:15
  993.3 65.5 %all-reduce.5.cloned.1.call-done = f32[512,64]{0,1:T(8,128)} async-done(((f32[512,64]{0,1:T(8,128)}), f32[512,64]{0,1:T(8,128)}) %all-reduce.5.cloned.1.call-update) | async-done | bytes 131088 | tf_op jit(solution)/shard_map/while/body/eval_jaxpr/psum | solution.py:15
  1077.1 65.8 %all-reduce.5.cloned.1.call-done = f32[512,64]{0,1:T(8,128)} async-done(((f32[512,64]{0,1:T(8,128)}), f32[512,64]{0,1:T(8,128)}) %all-reduce.5.cloned.1.call-update) | async-done | bytes 131088 | tf_op jit(solution)/shard_map/while/body/eval_jaxpr/psum | solution.py:15
  1150.5 5.9 collective-permute-start
  1161.2 65.5 %all-reduce.5.cloned.1.call-done = f32[512,64]{0,1:T(8,128)} async-done(((f32[512,64]{0,1:T(8,128)}), f32[512,64]{0,1:T(8,128)}) %all-reduce.5.cloned.1.call-update) | async-done | bytes 131088 | tf_op jit(solution)/shard_map/while/body/eval_jaxpr/psum | solution.py:15
  1234.3 5.9 collective-permute-start
  1245.0 65.6 %all-reduce.5.cloned.1.call-done = f32[512,64]{0,1:T(8,128)} async-done(((f32[512,64]{0,1:T(8,128)}), f32[512,64]{0,1:T(8,128)}) %all-reduce.5.cloned.1.call-update) | async-done | bytes 131088 | tf_op jit(solution)/shard_map/while/body/eval_jaxpr/psum | solution.py:15
  1318.1 5.9 collective-permute-start
  1328.8 65.5 %all-reduce.5.cloned.1.call-done = f32[512,64]{0,1:T(8,128)} async-done(((f32[512,64]{0,1:T(8,128)}), f32[512,64]{0,1:T(8,128)}) %all-reduce.5.cloned.1.call-update) | async-done | bytes 131088 | tf_op jit(solution)/shard_map/while/body/eval_jaxpr/psum | solution.py:15
  1402.7 74.8 %all-reduce.3.cloned.1.call-done = f32[512,64]{0,1:T(8,128)} async-done(((f32[512,64]{0,1:T(8,128)}), f32[512,64]{0,1:T(8,128)}) %all-reduce.3.cloned.1.call-update) | async-done | bytes 131088 | tf_op jit(solution)/shard_map/psum | solution.py:15
  1480.5 27.6 %psum.26 = f32[17,2]{1,0:T(8,128)S(1)} all-reduce(f32[17,2]{1,0:T(8,128)S(1)} %scatter.7), channel_id=1, replica_groups=mesh['skill'=64,'tensor'=8] {'tensor'}, use_global_device_ids=true, to_apply=%region_12.13 | all-reduce | flops 34 | bytes 272 | tf_op jit(solution)/shard_map/psum | solution.py:67
  (249 shorter events, 250.8 us)
Async XLA Ops:
  52.8 82.3 %all-reduce.5.cloned.1.call-start = ((), (), s32[]{:S(2)}) async-start(), calls=%async_computation.1 | async-start | bytes 262144 | tf_op jit(solution)/shard_map/while/body/eval_jaxpr/psum | solution.py:15
  56.2 83.3 %collective-permute-start = (bf16[1024,64]{1,0:T(8,128)(2,1)S(1)}, bf16[1024,64]{1,0:T(8,128)(2,1)}, u32[]{:S(2)}, u32[]{:S(2)}) collective-permute-start(bf16[1024,64]{1,0:T(8,128)(2,1)S(1)} %copy.20), channel_id=1, source_target_pairs={{8,0},{16,8},{24,16},{32,24},{40,32},{48,40},{56,48},{64,56},{72,6... | collective-permute-start | bytes 393224 | tf_op jit(solution)/shard_map/while/body/eval_jaxpr/ppermute | solution.py:10
  139.4 79.8 %all-reduce.5.cloned.1.call-start = ((), (), s32[]{:S(2)}) async-start(), calls=%async_computation.1 | async-start | bytes 262144 | tf_op jit(solution)/shard_map/while/body/eval_jaxpr/psum | solution.py:15
  142.8 80.7 %collective-permute-start = (bf16[1024,64]{1,0:T(8,128)(2,1)S(1)}, bf16[1024,64]{1,0:T(8,128)(2,1)}, u32[]{:S(2)}, u32[]{:S(2)}) collective-permute-start(bf16[1024,64]{1,0:T(8,128)(2,1)S(1)} %copy.20), channel_id=1, source_target_pairs={{8,0},{16,8},{24,16},{32,24},{40,32},{48,40},{56,48},{64,56},{72,6... | collective-permute-start | bytes 393224 | tf_op jit(solution)/shard_map/while/body/eval_jaxpr/ppermute | solution.py:10
  223.5 79.9 %all-reduce.5.cloned.1.call-start = ((), (), s32[]{:S(2)}) async-start(), calls=%async_computation.1 | async-start | bytes 262144 | tf_op jit(solution)/shard_map/while/body/eval_jaxpr/psum | solution.py:15
  226.9 80.8 %collective-permute-start = (bf16[1024,64]{1,0:T(8,128)(2,1)S(1)}, bf16[1024,64]{1,0:T(8,128)(2,1)}, u32[]{:S(2)}, u32[]{:S(2)}) collective-permute-start(bf16[1024,64]{1,0:T(8,128)(2,1)S(1)} %copy.20), channel_id=1, source_target_pairs={{8,0},{16,8},{24,16},{32,24},{40,32},{48,40},{56,48},{64,56},{72,6... | collective-permute-start | bytes 393224 | tf_op jit(solution)/shard_map/while/body/eval_jaxpr/ppermute | solution.py:10
  307.7 79.5 %all-reduce.5.cloned.1.call-start = ((), (), s32[]{:S(2)}) async-start(), calls=%async_computation.1 | async-start | bytes 262144 | tf_op jit(solution)/shard_map/while/body/eval_jaxpr/psum | solution.py:15
  311.0 80.4 %collective-permute-start = (bf16[1024,64]{1,0:T(8,128)(2,1)S(1)}, bf16[1024,64]{1,0:T(8,128)(2,1)}, u32[]{:S(2)}, u32[]{:S(2)}) collective-permute-start(bf16[1024,64]{1,0:T(8,128)(2,1)S(1)} %copy.20), channel_id=1, source_target_pairs={{8,0},{16,8},{24,16},{32,24},{40,32},{48,40},{56,48},{64,56},{72,6... | collective-permute-start | bytes 393224 | tf_op jit(solution)/shard_map/while/body/eval_jaxpr/ppermute | solution.py:10
  391.5 79.5 %all-reduce.5.cloned.1.call-start = ((), (), s32[]{:S(2)}) async-start(), calls=%async_computation.1 | async-start | bytes 262144 | tf_op jit(solution)/shard_map/while/body/eval_jaxpr/psum | solution.py:15
  394.8 80.4 %collective-permute-start = (bf16[1024,64]{1,0:T(8,128)(2,1)S(1)}, bf16[1024,64]{1,0:T(8,128)(2,1)}, u32[]{:S(2)}, u32[]{:S(2)}) collective-permute-start(bf16[1024,64]{1,0:T(8,128)(2,1)S(1)} %copy.20), channel_id=1, source_target_pairs={{8,0},{16,8},{24,16},{32,24},{40,32},{48,40},{56,48},{64,56},{72,6... | collective-permute-start | bytes 393224 | tf_op jit(solution)/shard_map/while/body/eval_jaxpr/ppermute | solution.py:10
  475.3 79.5 %all-reduce.5.cloned.1.call-start = ((), (), s32[]{:S(2)}) async-start(), calls=%async_computation.1 | async-start | bytes 262144 | tf_op jit(solution)/shard_map/while/body/eval_jaxpr/psum | solution.py:15
  478.6 80.4 %collective-permute-start = (bf16[1024,64]{1,0:T(8,128)(2,1)S(1)}, bf16[1024,64]{1,0:T(8,128)(2,1)}, u32[]{:S(2)}, u32[]{:S(2)}) collective-permute-start(bf16[1024,64]{1,0:T(8,128)(2,1)S(1)} %copy.20), channel_id=1, source_target_pairs={{8,0},{16,8},{24,16},{32,24},{40,32},{48,40},{56,48},{64,56},{72,6... | collective-permute-start | bytes 393224 | tf_op jit(solution)/shard_map/while/body/eval_jaxpr/ppermute | solution.py:10
  559.1 79.8 %all-reduce.5.cloned.1.call-start = ((), (), s32[]{:S(2)}) async-start(), calls=%async_computation.1 | async-start | bytes 262144 | tf_op jit(solution)/shard_map/while/body/eval_jaxpr/psum | solution.py:15
  562.4 80.7 %collective-permute-start = (bf16[1024,64]{1,0:T(8,128)(2,1)S(1)}, bf16[1024,64]{1,0:T(8,128)(2,1)}, u32[]{:S(2)}, u32[]{:S(2)}) collective-permute-start(bf16[1024,64]{1,0:T(8,128)(2,1)S(1)} %copy.20), channel_id=1, source_target_pairs={{8,0},{16,8},{24,16},{32,24},{40,32},{48,40},{56,48},{64,56},{72,6... | collective-permute-start | bytes 393224 | tf_op jit(solution)/shard_map/while/body/eval_jaxpr/ppermute | solution.py:10
  643.1 79.8 %all-reduce.5.cloned.1.call-start = ((), (), s32[]{:S(2)}) async-start(), calls=%async_computation.1 | async-start | bytes 262144 | tf_op jit(solution)/shard_map/while/body/eval_jaxpr/psum | solution.py:15
  646.5 80.7 %collective-permute-start = (bf16[1024,64]{1,0:T(8,128)(2,1)S(1)}, bf16[1024,64]{1,0:T(8,128)(2,1)}, u32[]{:S(2)}, u32[]{:S(2)}) collective-permute-start(bf16[1024,64]{1,0:T(8,128)(2,1)S(1)} %copy.20), channel_id=1, source_target_pairs={{8,0},{16,8},{24,16},{32,24},{40,32},{48,40},{56,48},{64,56},{72,6... | collective-permute-start | bytes 393224 | tf_op jit(solution)/shard_map/while/body/eval_jaxpr/ppermute | solution.py:10
  727.2 79.8 %all-reduce.5.cloned.1.call-start = ((), (), s32[]{:S(2)}) async-start(), calls=%async_computation.1 | async-start | bytes 262144 | tf_op jit(solution)/shard_map/while/body/eval_jaxpr/psum | solution.py:15
  730.6 80.7 %collective-permute-start = (bf16[1024,64]{1,0:T(8,128)(2,1)S(1)}, bf16[1024,64]{1,0:T(8,128)(2,1)}, u32[]{:S(2)}, u32[]{:S(2)}) collective-permute-start(bf16[1024,64]{1,0:T(8,128)(2,1)S(1)} %copy.20), channel_id=1, source_target_pairs={{8,0},{16,8},{24,16},{32,24},{40,32},{48,40},{56,48},{64,56},{72,6... | collective-permute-start | bytes 393224 | tf_op jit(solution)/shard_map/while/body/eval_jaxpr/ppermute | solution.py:10
  811.3 79.6 %all-reduce.5.cloned.1.call-start = ((), (), s32[]{:S(2)}) async-start(), calls=%async_computation.1 | async-start | bytes 262144 | tf_op jit(solution)/shard_map/while/body/eval_jaxpr/psum | solution.py:15
  814.7 80.5 %collective-permute-start = (bf16[1024,64]{1,0:T(8,128)(2,1)S(1)}, bf16[1024,64]{1,0:T(8,128)(2,1)}, u32[]{:S(2)}, u32[]{:S(2)}) collective-permute-start(bf16[1024,64]{1,0:T(8,128)(2,1)S(1)} %copy.20), channel_id=1, source_target_pairs={{8,0},{16,8},{24,16},{32,24},{40,32},{48,40},{56,48},{64,56},{72,6... | collective-permute-start | bytes 393224 | tf_op jit(solution)/shard_map/while/body/eval_jaxpr/ppermute | solution.py:10
  895.2 79.8 %all-reduce.5.cloned.1.call-start = ((), (), s32[]{:S(2)}) async-start(), calls=%async_computation.1 | async-start | bytes 262144 | tf_op jit(solution)/shard_map/while/body/eval_jaxpr/psum | solution.py:15
  898.5 80.7 %collective-permute-start = (bf16[1024,64]{1,0:T(8,128)(2,1)S(1)}, bf16[1024,64]{1,0:T(8,128)(2,1)}, u32[]{:S(2)}, u32[]{:S(2)}) collective-permute-start(bf16[1024,64]{1,0:T(8,128)(2,1)S(1)} %copy.20), channel_id=1, source_target_pairs={{8,0},{16,8},{24,16},{32,24},{40,32},{48,40},{56,48},{64,56},{72,6... | collective-permute-start | bytes 393224 | tf_op jit(solution)/shard_map/while/body/eval_jaxpr/ppermute | solution.py:10
  979.3 79.5 %all-reduce.5.cloned.1.call-start = ((), (), s32[]{:S(2)}) async-start(), calls=%async_computation.1 | async-start | bytes 262144 | tf_op jit(solution)/shard_map/while/body/eval_jaxpr/psum | solution.py:15
  982.6 80.4 %collective-permute-start = (bf16[1024,64]{1,0:T(8,128)(2,1)S(1)}, bf16[1024,64]{1,0:T(8,128)(2,1)}, u32[]{:S(2)}, u32[]{:S(2)}) collective-permute-start(bf16[1024,64]{1,0:T(8,128)(2,1)S(1)} %copy.20), channel_id=1, source_target_pairs={{8,0},{16,8},{24,16},{32,24},{40,32},{48,40},{56,48},{64,56},{72,6... | collective-permute-start | bytes 393224 | tf_op jit(solution)/shard_map/while/body/eval_jaxpr/ppermute | solution.py:10
  1063.1 79.8 %all-reduce.5.cloned.1.call-start = ((), (), s32[]{:S(2)}) async-start(), calls=%async_computation.1 | async-start | bytes 262144 | tf_op jit(solution)/shard_map/while/body/eval_jaxpr/psum | solution.py:15
  1066.4 80.7 %collective-permute-start = (bf16[1024,64]{1,0:T(8,128)(2,1)S(1)}, bf16[1024,64]{1,0:T(8,128)(2,1)}, u32[]{:S(2)}, u32[]{:S(2)}) collective-permute-start(bf16[1024,64]{1,0:T(8,128)(2,1)S(1)} %copy.20), channel_id=1, source_target_pairs={{8,0},{16,8},{24,16},{32,24},{40,32},{48,40},{56,48},{64,56},{72,6... | collective-permute-start | bytes 393224 | tf_op jit(solution)/shard_map/while/body/eval_jaxpr/ppermute | solution.py:10
  1147.2 79.5 %all-reduce.5.cloned.1.call-start = ((), (), s32[]{:S(2)}) async-start(), calls=%async_computation.1 | async-start | bytes 262144 | tf_op jit(solution)/shard_map/while/body/eval_jaxpr/psum | solution.py:15
  1150.5 80.4 %collective-permute-start = (bf16[1024,64]{1,0:T(8,128)(2,1)S(1)}, bf16[1024,64]{1,0:T(8,128)(2,1)}, u32[]{:S(2)}, u32[]{:S(2)}) collective-permute-start(bf16[1024,64]{1,0:T(8,128)(2,1)S(1)} %copy.20), channel_id=1, source_target_pairs={{8,0},{16,8},{24,16},{32,24},{40,32},{48,40},{56,48},{64,56},{72,6... | collective-permute-start | bytes 393224 | tf_op jit(solution)/shard_map/while/body/eval_jaxpr/ppermute | solution.py:10
  1230.9 79.6 %all-reduce.5.cloned.1.call-start = ((), (), s32[]{:S(2)}) async-start(), calls=%async_computation.1 | async-start | bytes 262144 | tf_op jit(solution)/shard_map/while/body/eval_jaxpr/psum | solution.py:15
  1234.3 80.5 %collective-permute-start = (bf16[1024,64]{1,0:T(8,128)(2,1)S(1)}, bf16[1024,64]{1,0:T(8,128)(2,1)}, u32[]{:S(2)}, u32[]{:S(2)}) collective-permute-start(bf16[1024,64]{1,0:T(8,128)(2,1)S(1)} %copy.20), channel_id=1, source_target_pairs={{8,0},{16,8},{24,16},{32,24},{40,32},{48,40},{56,48},{64,56},{72,6... | collective-permute-start | bytes 393224 | tf_op jit(solution)/shard_map/while/body/eval_jaxpr/ppermute | solution.py:10
  1314.8 79.5 %all-reduce.5.cloned.1.call-start = ((), (), s32[]{:S(2)}) async-start(), calls=%async_computation.1 | async-start | bytes 262144 | tf_op jit(solution)/shard_map/while/body/eval_jaxpr/psum | solution.py:15
  1318.1 80.4 %collective-permute-start = (bf16[1024,64]{1,0:T(8,128)(2,1)S(1)}, bf16[1024,64]{1,0:T(8,128)(2,1)}, u32[]{:S(2)}, u32[]{:S(2)}) collective-permute-start(bf16[1024,64]{1,0:T(8,128)(2,1)S(1)} %copy.20), channel_id=1, source_target_pairs={{8,0},{16,8},{24,16},{32,24},{40,32},{48,40},{56,48},{64,56},{72,6... | collective-permute-start | bytes 393224 | tf_op jit(solution)/shard_map/while/body/eval_jaxpr/ppermute | solution.py:10
  (24 other events, 1361.3 us)
Sparse Core Ops, SparseCore 0:
  56.8 78.2 all-reduce.4
  143.4 75.7 all-reduce.4
  227.5 75.8 all-reduce.4
  311.4 75.7 all-reduce.4
  395.2 75.7 all-reduce.4
  479.0 75.7 all-reduce.4
  563.0 75.7 all-reduce.4
  647.1 75.7 all-reduce.4
  731.2 75.7 all-reduce.4
  815.0 75.8 all-reduce.4
  899.2 75.7 all-reduce.4
  983.0 75.7 all-reduce.4
  1067.1 75.7 all-reduce.4
  1150.8 75.7 all-reduce.4
  1234.6 75.8 all-reduce.4
  1318.5 75.7 all-reduce.4
Sparse Core Ops, SparseCore 1:
  1402.0 75.5 all-reduce.2
